TPU v7x, 256 devices: a whole 4x4x8 slice. The times are simulated.
256 devices in a mesh: lon: 32 (over x_lo, z, core), lat: 8 (over x_hi, y).
Axes of the slice: x: 4 (x_hi: 2, x_lo: 2; x = x_hi * 2 + x_lo), y: 4, z: 8, core: 2. Of those that a mesh axis runs over, the one named last changes fastest.
Arguments:
- cotangent: bfloat16 [1440, 160, 1024], P('lon', None, 'lat'), may hold values from -6 to 6
- winds: bfloat16 [1440, 64, 1024], P('lon', None, 'lat'), may hold values from -0.44921875 to 0.44921875
- filter_ops: bfloat16 [16, 1440, 1440], P('lat', 'lon'), may hold values from -0.3125 to 0.3125
- block_band: int32 [16], replicated, may hold values from 0 to 7, as said below
- block_row: int32 [16], replicated, may hold values from 0 to 127
Outputs:
- adjoint_state: float32 [1440, 160, 1024], P('lon', None, 'lat')
Inputs may be any that keep to these rules, and one draw needn't show every extreme that they name: `block_band`: band 0 and band 8 - 1 each read exactly 5 blocks; the remaining blocks are spread over the other bands as evenly as possible, in an order drawn from the seed.
All inputs are finite; a program needn't handle non-finite values.
Results may differ from a plain program's by a relative error of at most 0.006.
Values may be sent and summed in bfloat16 or wider, within the bound.
No kernel may reach another device: no remote copies, remote signals or barrier semaphores. Data moves between devices by JAX's collectives and lax.ppermute only.
A program may use at most 128 MiB of HBM per device.

v0:
```python
import jax
import jax.numpy as jnp
from jax import lax
from jax.sharding import PartitionSpec as P

VAR = 5
LEV = 32
NSUB = 2


def padded(cells, sides, width, closed):
    for axis, dim in sides:
        count = lax.axis_size(axis)
        ends = count if closed else count - 1
        head = lax.slice_in_dim(cells, 0, width, axis=dim)
        tail = lax.slice_in_dim(cells, cells.shape[dim] - width, cells.shape[dim], axis=dim)
        cells = jnp.concatenate(
            [
                lax.ppermute(tail, axis, [(i, (i + 1) % count) for i in range(ends)]),
                cells,
                lax.ppermute(head, axis, [((i + 1) % count, i) for i in range(ends)]),
            ],
            axis=dim,
        )
    return cells


def rims(values):
    cycle_cells = padded(values, (("lon", 0),), 1, True)
    band_cells = padded(values, (("lat", 2),), 1, False)
    return (cycle_cells, band_cells)


def spread(coef):
    return jnp.tile(coef, (1, VAR, 1))


def filter_rows(slot_ops, picked):
    return lax.psum_scatter(
        jnp.einsum("kji,kjc->ikc", slot_ops, picked, preferred_element_type=jnp.float32),
        "lon",
        scatter_dimension=0,
        tiled=True,
    )


def shards(cotangent, winds, filter_ops, block_band, block_row):
    rows_here = cotangent.shape[2]
    band_total = lax.axis_size("lat")
    band_index = lax.axis_index("lat")
    wind_cycle, wind_band = rims(winds)
    courant_x = winds[:, :LEV, :].astype(jnp.float32)
    west_x = wind_cycle[:-2, :LEV, :].astype(jnp.float32)
    global_rows = band_index * rows_here - 1 + jnp.arange(rows_here + 2, dtype=jnp.int32)
    inside = (global_rows < band_total * rows_here - 1).astype(jnp.float32)[None, None, :]
    courant_y = wind_band[:, LEV:, :].astype(jnp.float32) * inside
    east_coef = spread(jnp.maximum(courant_x, 0.0))
    west_coef = spread(jnp.minimum(west_x, 0.0))
    north_coef = spread(jnp.maximum(courant_y[:, :, 1:-1], 0.0))
    south_coef = spread(jnp.minimum(courant_y[:, :, :-2], 0.0))
    owned_here = block_band == band_index
    row_match = block_row[:, None] == jnp.arange(rows_here, dtype=jnp.int32)[None, :]
    slot_count = filter_ops.shape[0] * (band_total + 2) // 4
    order_rank = jnp.cumsum(owned_here.astype(jnp.int32)) - 1
    chosen = owned_here[None, :] & (
        order_rank[None, :] == jnp.arange(slot_count, dtype=jnp.int32)[:, None]
    )
    chosen_weights = chosen.astype(jnp.bfloat16)
    slot_ops = jnp.einsum(
        "pb,bji->pji",
        chosen_weights,
        lax.all_gather(filter_ops, "lat", axis=0, tiled=True),
        preferred_element_type=jnp.float32,
    ).astype(jnp.bfloat16)
    slot_rows = jnp.einsum("pb,bl->pl", chosen.astype(jnp.float32), row_match.astype(jnp.float32))
    send_weights = slot_rows.astype(jnp.bfloat16)
    adjoint = cotangent.astype(jnp.float32)
    for substep in range(NSUB):
        rounded = adjoint.astype(jnp.bfloat16)
        widened = lax.optimization_barrier(rounded).astype(jnp.float32)
        picked = jnp.einsum(
            "pl,xcl->pxc", send_weights, rounded, preferred_element_type=jnp.float32
        )
        picked = picked.astype(jnp.bfloat16)
        filtered = filter_rows(slot_ops, picked)
        correction = jnp.einsum("kl,xkc->xcl", slot_rows, filtered)
        smoothed = (widened + correction).astype(jnp.bfloat16)
        cycle_cells, band_cells = rims(smoothed)
        centre = lax.optimization_barrier(smoothed).astype(jnp.float32)
        east_side = cycle_cells[2:].astype(jnp.float32)
        west_side = cycle_cells[:-2].astype(jnp.float32)
        north_side = band_cells[:, :, 2:].astype(jnp.float32)
        south_side = band_cells[:, :, :-2].astype(jnp.float32)
        adjoint = (
            centre
            + east_coef * (east_side - centre)
            + west_coef * (centre - west_side)
            + north_coef * (north_side - centre)
            + south_coef * (centre - south_side)
        )
    return adjoint


def solution(mesh):
    return jax.shard_map(
        shards,
        mesh=mesh,
        in_specs=(P("lon", None, "lat"), P("lon", None, "lat"), P("lat", "lon", None), P(), P()),
        out_specs=P("lon", None, "lat"),
        check_vma=False,
    )
```

profile of v0, /device:TPU:6, one launch (start us, length us, event | category | flops | bytes accessed | tf_op | source)
XLA Modules:
  0.0 445.1 jit_solution(5854807081802948387)
XLA Ops:
  6.5 1.7 copy.51
  8.3 0.7 convert_bitcast_fusion
  9.2 0.8 fusion.11
  10.1 2.6 convolution_convert_fusion.1
  12.6 59.8 %all-gather.2.cloned.1.call-done = bf16[16,45,1440]{2,1,0:T(8,128)(2,1)} async-done(((bf16[2,45,1440]{2,1,0:T(8,128)(2,1)}), bf16[16,45,1440]{2,1,0:T(8,128)(2,1)}) %all-gather.2.cloned.1.call-update) | async-done | bytes 2073616 | tf_op jit(solution)/shard_map/all_gather | solution.py:72
  72.4 3.0 fusion.7
  75.4 1.0 copy-done.5
  76.5 3.0 convolution_bitcast_fusion.1
  79.5 9.3 %copy.55 = f32[1440,5,160]{2,1,0:T(8,128)} copy(f32[1440,5,160]{0,2,1:T(8,128)} %convolution_bitcast_fusion.1) | data formatting | bytes 9216000 | tf_op jit(solution)/shard_map/kji,kjc->ikc/transpose | solution.py:40
  88.9 1.0 copy-done.2
  89.9 0.6 slice.84
  90.9 0.4 copy.71
  91.3 4.2 collective-permute-start.4
  95.9 1.9 collective-permute-start.3
  97.8 7.3 %collective-permute-done.3 = bf16[45,64,1]{1,0,2:T(8,128)(2,1)S(1)} collective-permute-done((bf16[45,64,1]{1,0,2:T(8,128)(2,1)S(1)}, bf16[45,64,1]{1,0,2:T(8,128)(2,1)S(1)}, u32[]{:S(2)}, u32[]{:S(2)}) %collective-permute-start.3) | collective-permute-done | bytes 5792 | tf_op jit(solution)/shard_map/ppermute | solution.py:19
  105.1 0.4 copy.58
  105.6 1.2 copy.59
  106.8 1.5 convert_multiply_fusion
  108.3 1.2 slice_maximum_fusion
  109.4 113.7 %reduce-scatter.3.cloned.1.call-done = f32[45,5,160]{2,1,0:T(8,128)} async-done(((f32[1440,5,160]{2,1,0:T(8,128)}), f32[45,5,160]{2,1,0:T(8,128)}) %reduce-scatter.3.cloned.1.call-update) | async-done | bytes 144016 | tf_op jit(solution)/shard_map/reduce_scatter | solution.py:39
  223.1 2.5 add_convert_fusion.1
  225.7 2.5 fusion.31
  228.2 0.4 collective-permute-start
  228.8 2.9 copy.60
  231.6 2.3 copy.62
  233.9 3.4 collective-permute-start.6
  237.3 6.2 %collective-permute-start.5 = (bf16[45,160,1]{1,0,2:T(8,128)(2,1)}, bf16[45,160,1]{1,0,2:T(8,128)(2,1)}, u32[]{:S(2)}, u32[]{:S(2)}) collective-permute-start(bf16[45,160,1]{1,0,2:T(8,128)(2,1)} %copy.60), channel_id=1, source_target_pairs={{1,0},{2,1},{3,2},{4,3},{5,4},{6,5},{7,6},{9,8},{10,9},{11,10},{12... | collective-permute-start | bytes 43208 | tf_op jit(solution)/shard_map/ppermute | solution.py:21
  243.6 1.3 convert_maximum_fusion
  245.1 2.6 copy.61
  247.7 1.8 copy.63
  249.5 6.4 %fusion.3 = bf16[45,160,128]{2,1,0:T(8,128)(2,1)S(1)} fusion(bf16[45,160,128]{2,1,0:T(8,128)(2,1)S(1)} %add_convert_fusion.1, bf16[45,160,1]{2,1,0:T(8,128)(2,1)} %copy.63, bf16[45,160,1]{2,1,0:T(8,128)(2,1)} %copy.61, bf16[1,160,128]{2,1,0:T(8,128)(2,1)S(1)} %collective-permute-done.2, bf16[1,160,128]{2,1,0:T(8,128)(2,1)S(1)} %collective-permute-done, ...), kind=kLoop, calls=%fused_computation.23 | loop fusion | flops 27648000 | bytes 6746240 | tf_op jit(solution)/shard_map/convert_element_type | solution.py:79
  255.9 1.2 copy-done
  257.2 1.1 convolution_convert_fusion
  258.2 3.1 convolution_bitcast_fusion
  261.3 9.3 %copy.65 = f32[1440,5,160]{2,1,0:T(8,128)} copy(f32[1440,5,160]{0,2,1:T(8,128)} %convolution_bitcast_fusion) | data formatting | bytes 9216000 | tf_op jit(solution)/shard_map/kji,kjc->ikc/transpose | solution.py:40
  270.6 132.5 %reduce-scatter.5.cloned.1.call-done = f32[45,5,160]{2,1,0:T(8,128)} async-done(((f32[1440,5,160]{2,1,0:T(8,128)}), f32[45,5,160]{2,1,0:T(8,128)}) %reduce-scatter.5.cloned.1.call-update) | async-done | bytes 144016 | tf_op jit(solution)/shard_map/reduce_scatter | solution.py:39
  403.1 2.0 fusion.12
  405.1 0.5 add_convert_fusion
  405.6 0.5 collective-permute-start.7
  406.2 2.5 fusion.29
  408.7 2.3 copy.66
  411.0 5.8 %collective-permute-start.9 = (bf16[45,160,1]{1,0,2:T(8,128)(2,1)S(1)}, bf16[45,160,1]{1,0,2:T(8,128)(2,1)S(1)}, u32[]{:S(2)}, u32[]{:S(2)}) collective-permute-start(bf16[45,160,1]{1,0,2:T(8,128)(2,1)S(1)} %copy.66), channel_id=1, source_target_pairs={{1,0},{2,1},{3,2},{4,3},{5,4},{6,5},{7,6},{9,8},{10,9},{11,10},{12... | collective-permute-start | bytes 43208 | tf_op jit(solution)/shard_map/ppermute | solution.py:21
  416.9 2.3 copy.68
  419.1 1.9 collective-permute-start.10
  421.1 1.8 copy.67
  422.9 5.7 %collective-permute-done.10 = bf16[45,160,1]{1,0,2:T(8,128)(2,1)} collective-permute-done((bf16[45,160,1]{1,0,2:T(8,128)(2,1)S(1)}, bf16[45,160,1]{1,0,2:T(8,128)(2,1)}, u32[]{:S(2)}, u32[]{:S(2)}) %collective-permute-start.10) | collective-permute-done | bytes 14432 | tf_op jit(solution)/shard_map/ppermute | solution.py:19
  428.6 2.6 copy.69
  431.1 7.4 %fusion.6 = f32[45,160,128]{2,1,0:T(8,128)} fusion(bf16[45,160,128]{2,1,0:T(8,128)(2,1)S(1)} %add_convert_fusion, bf16[45,160,1]{2,1,0:T(8,128)(2,1)} %copy.69, bf16[45,160,1]{2,1,0:T(8,128)(2,1)} %copy.67, bf16[1,160,128]{2,1,0:T(8,128)(2,1)S(1)} %collective-permute-done.8, bf16[1,160,128]{2,1,0:T(8,128)(2,1)S(1)} %collective-permute-done.7, ...), kind=kLoop, calls=%fused_computation.26 | loop fusion | flops 26726400 | bytes 8589440 | tf_op jit(solution)/shard_map/add | solution.py:95
  (37 shorter events, 1.5 us)
Async XLA Ops:
  6.5 65.9 %all-gather.2.cloned.1.call-start = ((), (), s32[]{:S(2)}) async-start(), calls=%async_computation.2 | async-start | bytes 2654208 | tf_op jit(solution)/shard_map/all_gather | solution.py:72
  8.3 214.9 %reduce-scatter.3.cloned.1.call-start = ((), (), s32[]{:S(2)}) async-start(), calls=%async_computation.3 | async-start | bytes 12165120 | tf_op jit(solution)/shard_map/reduce_scatter | solution.py:39
  75.4 1.0 copy-start.5
  88.8 1.1 copy-start.2
  88.9 314.2 %reduce-scatter.5.cloned.1.call-start = ((), (), s32[]{:S(2)}) async-start(), calls=%async_computation.4 | async-start | bytes 12165120 | tf_op jit(solution)/shard_map/reduce_scatter | solution.py:39
  90.5 153.0 %collective-permute-start.1 = (bf16[1,64,128]{2,1,0:T(8,128)(2,1)}, bf16[1,64,128]{2,1,0:T(8,128)(2,1)S(1)}, u32[]{:S(2)}, u32[]{:S(2)}) collective-permute-start(bf16[1,64,128]{2,1,0:T(8,128)(2,1)} %slice.84), channel_id=1, source_target_pairs={{0,8},{8,16},{16,24},{24,32},{32,40},{40,48},{48,56},{56,64},{64,7... | collective-permute-start | bytes 49160 | tf_op jit(solution)/shard_map/ppermute | solution.py:19
  91.3 14.3 %collective-permute-start.4 = (bf16[45,64,1]{1,0,2:T(8,128)(2,1)S(1)}, bf16[45,64,1]{1,0,2:T(8,128)(2,1)S(1)}, u32[]{:S(2)}, u32[]{:S(2)}) collective-permute-start(bf16[45,64,1]{1,0,2:T(8,128)(2,1)S(1)} %copy.71), channel_id=1, source_target_pairs={{1,0},{2,1},{3,2},{4,3},{5,4},{6,5},{7,6},{9,8},{10,9},{11,10},{12... | collective-permute-start | bytes 17288 | tf_op jit(solution)/shard_map/ppermute | solution.py:21
  95.9 9.2 %collective-permute-start.3 = (bf16[45,64,1]{1,0,2:T(8,128)(2,1)S(1)}, bf16[45,64,1]{1,0,2:T(8,128)(2,1)S(1)}, u32[]{:S(2)}, u32[]{:S(2)}) collective-permute-start(bf16[45,64,1]{1,0,2:T(8,128)(2,1)S(1)} %copy.70), channel_id=1, source_target_pairs={{0,1},{1,2},{2,3},{3,4},{4,5},{5,6},{6,7},{8,9},{9,10},{10,11},{11... | collective-permute-start | bytes 17288 | tf_op jit(solution)/shard_map/ppermute | solution.py:19
  228.2 21.3 %collective-permute-start = (bf16[1,160,128]{2,1,0:T(8,128)(2,1)S(1)}, bf16[1,160,128]{2,1,0:T(8,128)(2,1)S(1)}, u32[]{:S(2)}, u32[]{:S(2)}) collective-permute-start(bf16[1,160,128]{2,1,0:T(8,128)(2,1)S(1)} %get-tuple-element.11), channel_id=1, source_target_pairs={{8,0},{16,8},{24,16},{32,24},{40,32},{48,40},{56,48},{64,56},{72,6... | collective-permute-start | bytes 122888 | tf_op jit(solution)/shard_map/ppermute | solution.py:21
  228.6 20.9 %collective-permute-start.2 = (bf16[1,160,128]{2,1,0:T(8,128)(2,1)S(1)}, bf16[1,160,128]{2,1,0:T(8,128)(2,1)S(1)}, u32[]{:S(2)}, u32[]{:S(2)}) collective-permute-start(bf16[1,160,128]{2,1,0:T(8,128)(2,1)S(1)} %get-tuple-element.12), channel_id=1, source_target_pairs={{0,8},{8,16},{16,24},{24,32},{32,40},{40,48},{48,56},{56,64},{64,7... | collective-permute-start | bytes 122888 | tf_op jit(solution)/shard_map/ppermute | solution.py:19
  233.9 13.8 %collective-permute-start.6 = (bf16[45,160,1]{1,0,2:T(8,128)(2,1)S(1)}, bf16[45,160,1]{1,0,2:T(8,128)(2,1)S(1)}, u32[]{:S(2)}, u32[]{:S(2)}) collective-permute-start(bf16[45,160,1]{1,0,2:T(8,128)(2,1)S(1)} %copy.62), channel_id=1, source_target_pairs={{0,1},{1,2},{2,3},{3,4},{4,5},{5,6},{6,7},{8,9},{9,10},{10,11},{11... | collective-permute-start | bytes 43208 | tf_op jit(solution)/shard_map/ppermute | solution.py:19
  237.3 7.8 %collective-permute-start.5 = (bf16[45,160,1]{1,0,2:T(8,128)(2,1)}, bf16[45,160,1]{1,0,2:T(8,128)(2,1)}, u32[]{:S(2)}, u32[]{:S(2)}) collective-permute-start(bf16[45,160,1]{1,0,2:T(8,128)(2,1)} %copy.60), channel_id=1, source_target_pairs={{1,0},{2,1},{3,2},{4,3},{5,4},{6,5},{7,6},{9,8},{10,9},{11,10},{12... | collective-permute-start | bytes 43208 | tf_op jit(solution)/shard_map/ppermute | solution.py:21
  244.9 4.6 %copy-start.3 = (f32[45,32,128]{2,1,0:T(8,128)S(1)}, f32[45,32,128]{2,1,0:T(8,128)}, u32[]{:S(2)}) copy-start(f32[45,32,128]{2,1,0:T(8,128)} %get-tuple-element.16) | copy-start | bytes 2211844
  249.5 8.7 %copy-start.6 = (bf16[5,45,1440]{2,0,1:T(8,128)(2,1)S(1)}, bf16[5,45,1440]{2,0,1:T(8,128)(2,1)}, u32[]{:S(2)}) copy-start(bf16[5,45,1440]{2,0,1:T(8,128)(2,1)} %copy-done.5) | copy-start | bytes 1944004
  255.9 1.2 copy-start
  403.1 2.0 copy-start.1
  405.6 25.5 %collective-permute-start.7 = (bf16[1,160,128]{2,1,0:T(8,128)(2,1)S(1)}, bf16[1,160,128]{2,1,0:T(8,128)(2,1)S(1)}, u32[]{:S(2)}, u32[]{:S(2)}) collective-permute-start(bf16[1,160,128]{2,1,0:T(8,128)(2,1)S(1)} %get-tuple-element.7), channel_id=1, source_target_pairs={{8,0},{16,8},{24,16},{32,24},{40,32},{48,40},{56,48},{64,56},{72,6... | collective-permute-start | bytes 122888 | tf_op jit(solution)/shard_map/ppermute | solution.py:21
  406.1 25.0 %collective-permute-start.8 = (bf16[1,160,128]{2,1,0:T(8,128)(2,1)S(1)}, bf16[1,160,128]{2,1,0:T(8,128)(2,1)S(1)}, u32[]{:S(2)}, u32[]{:S(2)}) collective-permute-start(bf16[1,160,128]{2,1,0:T(8,128)(2,1)S(1)} %get-tuple-element.8), channel_id=1, source_target_pairs={{0,8},{8,16},{16,24},{24,32},{32,40},{40,48},{48,56},{56,64},{64,7... | collective-permute-start | bytes 122888 | tf_op jit(solution)/shard_map/ppermute | solution.py:19
  408.7 22.5 %copy-start.4 = (f32[45,32,128]{2,1,0:T(8,128)S(1)}, f32[45,32,128]{2,1,0:T(8,128)}, u32[]{:S(2)}) copy-start(f32[45,32,128]{2,1,0:T(8,128)} %get-tuple-element.16) | copy-start | bytes 2211844
  411.0 10.0 %collective-permute-start.9 = (bf16[45,160,1]{1,0,2:T(8,128)(2,1)S(1)}, bf16[45,160,1]{1,0,2:T(8,128)(2,1)S(1)}, u32[]{:S(2)}, u32[]{:S(2)}) collective-permute-start(bf16[45,160,1]{1,0,2:T(8,128)(2,1)S(1)} %copy.66), channel_id=1, source_target_pairs={{1,0},{2,1},{3,2},{4,3},{5,4},{6,5},{7,6},{9,8},{10,9},{11,10},{12... | collective-permute-start | bytes 43208 | tf_op jit(solution)/shard_map/ppermute | solution.py:21
  419.1 9.4 %collective-permute-start.10 = (bf16[45,160,1]{1,0,2:T(8,128)(2,1)S(1)}, bf16[45,160,1]{1,0,2:T(8,128)(2,1)}, u32[]{:S(2)}, u32[]{:S(2)}) collective-permute-start(bf16[45,160,1]{1,0,2:T(8,128)(2,1)S(1)} %copy.68), channel_id=1, source_target_pairs={{0,1},{1,2},{2,3},{3,4},{4,5},{5,6},{6,7},{8,9},{9,10},{10,11},{11... | collective-permute-start | bytes 43208 | tf_op jit(solution)/shard_map/ppermute | solution.py:19
Sparse Core Ops, SparseCore 0:
  9.9 62.4 all-gather.1
  89.0 134.1 reduce-scatter.2
  270.8 132.2 reduce-scatter.4
where the time goes:
time: 446 us; the launch traced here: 445 us
  waiting for transfers between devices  319 us (72%)
  local copies, waits for them, and re-layouts  50.6 us (11%)
  starting transfers between devices  24.8 us (6%)
  other arithmetic  19 us (4%)
  matrix products  18.1 us (4%)
  between operations  13.3 us (3%)
    reduce_scatter x2, waiting for transfers between devices, filter_rows(): lax.psum_scatter(jnp.einsum('kji,kjc->ikc', slot_ops, picked, preferred_e...  246 us
    all_gather x1, waiting for transfers between devices, shards(): lax.all_gather(filter_ops, 'lat', axis=0, tiled=True)  59.8 us
    transpose x2, local copies, waits for them, and re-layouts, filter_rows(): jnp.einsum('kji,kjc->ikc', slot_ops, picked, preferred_element_type=jnp.f...  18.7 us
    ppermute x5, starting transfers between devices, padded(): lax.ppermute(head, axis, [((i + 1) % count, i) for i in range(ends)])  17.3 us
    ppermute x6, waiting for transfers between devices, padded(): lax.ppermute(tail, axis, [(i, (i + 1) % count) for i in range(ends)])  12.9 us
    slice x6, local copies, waits for them, and re-layouts, padded(): head = lax.slice_in_dim(cells, 0, width, axis=dim)  10.2 us
  transfers between devices with their start and end apart: 14, of which 6 were waited for; matrix products, arithmetic and copies ran while one was open for 8% of the time, Pallas kernels for 0%

commit v1 on v0

--- a/solution.py
+++ b/solution.py
@@ -69,7 +69,9 @@
     slot_ops = jnp.einsum(
         "pb,bji->pji",
         chosen_weights,
-        lax.all_gather(filter_ops, "lat", axis=0, tiled=True),
+        jnp.concatenate(
+            lax.all_to_all(jnp.stack([filter_ops] * lax.axis_size("lat")), "lat", 0, 0), axis=0
+        ),
         preferred_element_type=jnp.float32,
     ).astype(jnp.bfloat16)
     slot_rows = jnp.einsum("pb,bl->pl", chosen.astype(jnp.float32), row_match.astype(jnp.float32))

time: 446 us -> 426 us (0.955)
  waiting for transfers between devices: 319 us -> 284 us
  local copies, waits for them, and re-layouts: 50.6 us -> 60.8 us
  starting transfers between devices: 24.8 us -> 33 us
    all_gather x1 -> x0, waiting for transfers between devices: 59.8 us -> none  [shards(): lax.all_gather(filter_ops, 'lat', axis=0, tiled=True)]
    all_to_all x0 -> x1, waiting for transfers between devices: none -> 23.7 us  [shards(): lax.all_to_all(jnp.stack([filter_ops] * lax.axis_size('lat')), 'lat', 0, 0)]
    all_to_all x0 -> x1, starting transfers between devices: none -> 7.43 us  [shards(): lax.all_to_all(jnp.stack([filter_ops] * lax.axis_size('lat')), 'lat', 0, 0)]
    reshape x0 -> x1, local copies, waits for them, and re-layouts: none -> 4.72 us  [shards(): jnp.concatenate(lax.all_to_all(jnp.stack([filter_ops] * lax.axis_size('la...]
  transfers between devices with their start and end apart: 14 -> 14, of which waited for: 6 -> 6; matrix products, arithmetic and copies ran while one was open for 8% -> 9% of each run, Pallas kernels for 0% -> 0%
where the time goes in v1:
time: 426 us; the launch traced here: 425 us
  waiting for transfers between devices  284 us (67%)
  local copies, waits for them, and re-layouts  60.8 us (14%)
  starting transfers between devices  33 us (8%)
  other arithmetic  18.4 us (4%)
  matrix products  14.9 us (3%)
  between operations  13.6 us (3%)
    reduce_scatter x2, waiting for transfers between devices, filter_rows(): lax.psum_scatter(jnp.einsum('kji,kjc->ikc', slot_ops, picked, preferred_e...  248 us
    all_to_all x1, waiting for transfers between devices, shards(): lax.all_to_all(jnp.stack([filter_ops] * lax.axis_size('lat')), 'lat', 0, 0)  23.7 us
    transpose x2, local copies, waits for them, and re-layouts, filter_rows(): jnp.einsum('kji,kjc->ikc', slot_ops, picked, preferred_element_type=jnp.f...  18.7 us
    ppermute x5, starting transfers between devices, padded(): lax.ppermute(head, axis, [((i + 1) % count, i) for i in range(ends)])  18 us
    ppermute x6, waiting for transfers between devices, padded(): lax.ppermute(tail, axis, [(i, (i + 1) % count) for i in range(ends)])  12.7 us
    slice x6, local copies, waits for them, and re-layouts, padded(): head = lax.slice_in_dim(cells, 0, width, axis=dim)  10.2 us
  transfers between devices with their start and end apart: 14, of which 6 were waited for; matrix products, arithmetic and copies ran while one was open for 9% of the time, Pallas kernels for 0%

profile of v1, /device:TPU:6, one launch (start us, length us, event | category | flops | bytes accessed | tf_op | source)
XLA Modules:
  0.0 425.1 jit_solution(16422232079049559882)
XLA Ops:
  6.5 3.5 stack.2
  10.0 7.4 %all-to-all-start = ((bf16[8,2,45,1440]{3,1,2,0:T(2,128)(2,1)}), bf16[8,2,45,1440]{3,1,2,0:T(2,128)(2,1)S(1)}, u32[]{:S(2)}, u32[]{:S(2)}) async-start(bf16[8,2,45,1440]{3,1,2,0:T(2,128)(2,1)} %stack.2), calls=%async_computation | async-start | bytes 4423680 | tf_op jit(solution)/shard_map/all_to_all | solution.py:73
  17.9 2.6 convolution_convert_fusion.1
  20.5 23.7 %all-to-all-done = bf16[8,2,45,1440]{3,1,2,0:T(2,128)(2,1)S(1)} async-done(((bf16[8,2,45,1440]{3,1,2,0:T(2,128)(2,1)}), bf16[8,2,45,1440]{3,1,2,0:T(2,128)(2,1)S(1)}, u32[]{:S(2)}, u32[]{:S(2)}) %all-to-all-start) | async-done | bytes 2073632 | tf_op jit(solution)/shard_map/all_to_all | solution.py:73
  44.2 3.7 copy.49
  47.9 4.7 %reshape.58 = bf16[16,45,1440]{2,0,1:T(8,128)(2,1)S(1)} reshape(bf16[8,2,45,1440]{3,1,0,2:T(2,128)(2,1)} %copy.49) | data formatting | bytes 4147200 | tf_op jit(solution)/shard_map/reshape | solution.py:72
  52.6 0.4 fusion.17
  53.1 1.0 copy-done.5
  54.1 3.0 convolution_bitcast_fusion.1
  57.1 9.3 %copy.52 = f32[1440,5,160]{2,1,0:T(8,128)} copy(f32[1440,5,160]{0,2,1:T(8,128)} %convolution_bitcast_fusion.1) | data formatting | bytes 9216000 | tf_op jit(solution)/shard_map/kji,kjc->ikc/transpose | solution.py:40
  66.5 1.0 copy-done.2
  67.6 0.6 slice.84
  68.9 5.3 %collective-permute-start.4 = (bf16[45,64,1]{1,0,2:T(8,128)(2,1)S(1)}, bf16[45,64,1]{1,0,2:T(8,128)(2,1)S(1)}, u32[]{:S(2)}, u32[]{:S(2)}) collective-permute-start(bf16[45,64,1]{1,0,2:T(8,128)(2,1)S(1)} %copy.68), channel_id=1, source_target_pairs={{1,0},{2,1},{3,2},{4,3},{5,4},{6,5},{7,6},{9,8},{10,9},{11,10},{12... | collective-permute-start | bytes 17288 | tf_op jit(solution)/shard_map/ppermute | solution.py:21
  74.6 1.9 collective-permute-start.3
  76.5 7.3 %collective-permute-done.3 = bf16[45,64,1]{1,0,2:T(8,128)(2,1)S(1)} collective-permute-done((bf16[45,64,1]{1,0,2:T(8,128)(2,1)S(1)}, bf16[45,64,1]{1,0,2:T(8,128)(2,1)S(1)}, u32[]{:S(2)}, u32[]{:S(2)}) %collective-permute-start.3) | collective-permute-done | bytes 5792 | tf_op jit(solution)/shard_map/ppermute | solution.py:19
  83.8 0.4 copy.55
  84.3 1.2 copy.56
  85.5 1.5 convert_multiply_fusion
  87.0 1.2 slice_maximum_fusion
  88.1 114.4 %reduce-scatter.3.cloned.1.call-done = f32[45,5,160]{2,1,0:T(8,128)} async-done(((f32[1440,5,160]{2,1,0:T(8,128)}), f32[45,5,160]{2,1,0:T(8,128)}) %reduce-scatter.3.cloned.1.call-update) | async-done | bytes 144016 | tf_op jit(solution)/shard_map/reduce_scatter | solution.py:39
  202.6 2.5 add_convert_fusion.1
  205.1 2.5 fusion.30
  207.6 0.7 collective-permute-start
  208.4 2.9 copy.57
  211.2 2.3 copy.59
  213.5 3.3 collective-permute-start.6
  216.8 6.1 %collective-permute-start.5 = (bf16[45,160,1]{1,0,2:T(8,128)(2,1)}, bf16[45,160,1]{1,0,2:T(8,128)(2,1)}, u32[]{:S(2)}, u32[]{:S(2)}) collective-permute-start(bf16[45,160,1]{1,0,2:T(8,128)(2,1)} %copy.57), channel_id=1, source_target_pairs={{1,0},{2,1},{3,2},{4,3},{5,4},{6,5},{7,6},{9,8},{10,9},{11,10},{12... | collective-permute-start | bytes 43208 | tf_op jit(solution)/shard_map/ppermute | solution.py:21
  223.0 1.3 convert_maximum_fusion
  224.7 2.5 copy.58
  227.2 1.8 copy.60
  229.1 6.4 %fusion.3 = bf16[45,160,128]{2,1,0:T(8,128)(2,1)S(1)} fusion(bf16[45,160,128]{2,1,0:T(8,128)(2,1)S(1)} %add_convert_fusion.1, bf16[45,160,1]{2,1,0:T(8,128)(2,1)} %copy.60, bf16[45,160,1]{2,1,0:T(8,128)(2,1)} %copy.58, bf16[1,160,128]{2,1,0:T(8,128)(2,1)S(1)} %collective-permute-done.2, bf16[1,160,128]{2,1,0:T(8,128)(2,1)S(1)} %collective-permute-done, ...), kind=kLoop, calls=%fused_computation.23 | loop fusion | flops 27648000 | bytes 6746240 | tf_op jit(solution)/shard_map/convert_element_type | solution.py:81
  235.5 1.2 copy-done
  236.7 1.1 convolution_convert_fusion
  237.7 3.1 convolution_bitcast_fusion
  240.8 9.3 %copy.62 = f32[1440,5,160]{2,1,0:T(8,128)} copy(f32[1440,5,160]{0,2,1:T(8,128)} %convolution_bitcast_fusion) | data formatting | bytes 9216000 | tf_op jit(solution)/shard_map/kji,kjc->ikc/transpose | solution.py:40
  250.2 133.1 %reduce-scatter.5.cloned.1.call-done = f32[45,5,160]{2,1,0:T(8,128)} async-done(((f32[1440,5,160]{2,1,0:T(8,128)}), f32[45,5,160]{2,1,0:T(8,128)}) %reduce-scatter.5.cloned.1.call-update) | async-done | bytes 144016 | tf_op jit(solution)/shard_map/reduce_scatter | solution.py:39
  383.3 2.0 fusion.10
  385.3 0.5 add_convert_fusion
  385.8 0.4 collective-permute-start.7
  386.4 2.5 fusion.28
  388.9 2.3 copy.63
  391.2 5.4 %collective-permute-start.9 = (bf16[45,160,1]{1,0,2:T(8,128)(2,1)S(1)}, bf16[45,160,1]{1,0,2:T(8,128)(2,1)S(1)}, u32[]{:S(2)}, u32[]{:S(2)}) collective-permute-start(bf16[45,160,1]{1,0,2:T(8,128)(2,1)S(1)} %copy.63), channel_id=1, source_target_pairs={{1,0},{2,1},{3,2},{4,3},{5,4},{6,5},{7,6},{9,8},{10,9},{11,10},{12... | collective-permute-start | bytes 43208 | tf_op jit(solution)/shard_map/ppermute | solution.py:21
  396.6 2.3 copy.65
  398.9 2.1 collective-permute-start.10
  401.0 1.8 copy.64
  402.9 5.4 %collective-permute-done.10 = bf16[45,160,1]{1,0,2:T(8,128)(2,1)} collective-permute-done((bf16[45,160,1]{1,0,2:T(8,128)(2,1)S(1)}, bf16[45,160,1]{1,0,2:T(8,128)(2,1)}, u32[]{:S(2)}, u32[]{:S(2)}) %collective-permute-start.10) | collective-permute-done | bytes 14432 | tf_op jit(solution)/shard_map/ppermute | solution.py:19
  408.3 2.5 copy.66
  410.9 7.4 %fusion.6 = f32[45,160,128]{2,1,0:T(8,128)} fusion(bf16[45,160,128]{2,1,0:T(8,128)(2,1)S(1)} %add_convert_fusion, bf16[45,160,1]{2,1,0:T(8,128)(2,1)} %copy.66, bf16[45,160,1]{2,1,0:T(8,128)(2,1)} %copy.64, bf16[1,160,128]{2,1,0:T(8,128)(2,1)S(1)} %collective-permute-done.8, bf16[1,160,128]{2,1,0:T(8,128)(2,1)S(1)} %collective-permute-done.7, ...), kind=kLoop, calls=%fused_computation.26 | loop fusion | flops 26726400 | bytes 8589440 | tf_op jit(solution)/shard_map/add | solution.py:97
  (42 shorter events, 2.2 us)
Async XLA Ops:
  6.5 10.9 %copy-start.7 = (s32[16]{0:T(128)S(1)}, s32[16]{0:T(128)}, u32[]{:S(2)}) copy-start(s32[16]{0:T(128)} %param.8) | copy-start | bytes 196
  6.5 11.2 %copy-start.8 = (s32[16]{0:T(128)S(1)}, s32[16]{0:T(128)}, u32[]{:S(2)}) copy-start(s32[16]{0:T(128)} %param.9) | copy-start | bytes 196
  10.0 34.1 %all-to-all-start = ((bf16[8,2,45,1440]{3,1,2,0:T(2,128)(2,1)}), bf16[8,2,45,1440]{3,1,2,0:T(2,128)(2,1)S(1)}, u32[]{:S(2)}, u32[]{:S(2)}) async-start(bf16[8,2,45,1440]{3,1,2,0:T(2,128)(2,1)} %stack.2), calls=%async_computation | async-start | bytes 4423680 | tf_op jit(solution)/shard_map/all_to_all | solution.py:73
  17.5 185.1 %reduce-scatter.3.cloned.1.call-start = ((), (), s32[]{:S(2)}) async-start(), calls=%async_computation.3 | async-start | bytes 12165120 | tf_op jit(solution)/shard_map/reduce_scatter | solution.py:39
  53.1 1.0 copy-start.5
  66.5 1.1 copy-start.2
  66.5 316.8 %reduce-scatter.5.cloned.1.call-start = ((), (), s32[]{:S(2)}) async-start(), calls=%async_computation.4 | async-start | bytes 12165120 | tf_op jit(solution)/shard_map/reduce_scatter | solution.py:39
  68.2 154.8 %collective-permute-start.1 = (bf16[1,64,128]{2,1,0:T(8,128)(2,1)}, bf16[1,64,128]{2,1,0:T(8,128)(2,1)S(1)}, u32[]{:S(2)}, u32[]{:S(2)}) collective-permute-start(bf16[1,64,128]{2,1,0:T(8,128)(2,1)} %slice.84), channel_id=1, source_target_pairs={{0,8},{8,16},{16,24},{24,32},{32,40},{40,48},{48,56},{56,64},{64,7... | collective-permute-start | bytes 49160 | tf_op jit(solution)/shard_map/ppermute | solution.py:19
  68.9 15.3 %collective-permute-start.4 = (bf16[45,64,1]{1,0,2:T(8,128)(2,1)S(1)}, bf16[45,64,1]{1,0,2:T(8,128)(2,1)S(1)}, u32[]{:S(2)}, u32[]{:S(2)}) collective-permute-start(bf16[45,64,1]{1,0,2:T(8,128)(2,1)S(1)} %copy.68), channel_id=1, source_target_pairs={{1,0},{2,1},{3,2},{4,3},{5,4},{6,5},{7,6},{9,8},{10,9},{11,10},{12... | collective-permute-start | bytes 17288 | tf_op jit(solution)/shard_map/ppermute | solution.py:21
  74.6 9.2 %collective-permute-start.3 = (bf16[45,64,1]{1,0,2:T(8,128)(2,1)S(1)}, bf16[45,64,1]{1,0,2:T(8,128)(2,1)S(1)}, u32[]{:S(2)}, u32[]{:S(2)}) collective-permute-start(bf16[45,64,1]{1,0,2:T(8,128)(2,1)S(1)} %copy.67), channel_id=1, source_target_pairs={{0,1},{1,2},{2,3},{3,4},{4,5},{5,6},{6,7},{8,9},{9,10},{10,11},{11... | collective-permute-start | bytes 17288 | tf_op jit(solution)/shard_map/ppermute | solution.py:19
  207.6 21.4 %collective-permute-start = (bf16[1,160,128]{2,1,0:T(8,128)(2,1)S(1)}, bf16[1,160,128]{2,1,0:T(8,128)(2,1)S(1)}, u32[]{:S(2)}, u32[]{:S(2)}) collective-permute-start(bf16[1,160,128]{2,1,0:T(8,128)(2,1)S(1)} %get-tuple-element.11), channel_id=1, source_target_pairs={{8,0},{16,8},{24,16},{32,24},{40,32},{48,40},{56,48},{64,56},{72,6... | collective-permute-start | bytes 122888 | tf_op jit(solution)/shard_map/ppermute | solution.py:21
  208.3 20.7 %collective-permute-start.2 = (bf16[1,160,128]{2,1,0:T(8,128)(2,1)S(1)}, bf16[1,160,128]{2,1,0:T(8,128)(2,1)S(1)}, u32[]{:S(2)}, u32[]{:S(2)}) collective-permute-start(bf16[1,160,128]{2,1,0:T(8,128)(2,1)S(1)} %get-tuple-element.12), channel_id=1, source_target_pairs={{0,8},{8,16},{16,24},{24,32},{32,40},{40,48},{48,56},{56,64},{64,7... | collective-permute-start | bytes 122888 | tf_op jit(solution)/shard_map/ppermute | solution.py:19
  213.5 13.7 %collective-permute-start.6 = (bf16[45,160,1]{1,0,2:T(8,128)(2,1)S(1)}, bf16[45,160,1]{1,0,2:T(8,128)(2,1)S(1)}, u32[]{:S(2)}, u32[]{:S(2)}) collective-permute-start(bf16[45,160,1]{1,0,2:T(8,128)(2,1)S(1)} %copy.59), channel_id=1, source_target_pairs={{0,1},{1,2},{2,3},{3,4},{4,5},{5,6},{6,7},{8,9},{9,10},{10,11},{11... | collective-permute-start | bytes 43208 | tf_op jit(solution)/shard_map/ppermute | solution.py:19
  216.8 7.9 %collective-permute-start.5 = (bf16[45,160,1]{1,0,2:T(8,128)(2,1)}, bf16[45,160,1]{1,0,2:T(8,128)(2,1)}, u32[]{:S(2)}, u32[]{:S(2)}) collective-permute-start(bf16[45,160,1]{1,0,2:T(8,128)(2,1)} %copy.57), channel_id=1, source_target_pairs={{1,0},{2,1},{3,2},{4,3},{5,4},{6,5},{7,6},{9,8},{10,9},{11,10},{12... | collective-permute-start | bytes 43208 | tf_op jit(solution)/shard_map/ppermute | solution.py:21
  224.3 4.7 %copy-start.3 = (f32[45,32,128]{2,1,0:T(8,128)S(1)}, f32[45,32,128]{2,1,0:T(8,128)}, u32[]{:S(2)}) copy-start(f32[45,32,128]{2,1,0:T(8,128)} %get-tuple-element.16) | copy-start | bytes 2211844
  229.0 8.7 %copy-start.6 = (bf16[5,45,1440]{2,0,1:T(8,128)(2,1)S(1)}, bf16[5,45,1440]{2,0,1:T(8,128)(2,1)}, u32[]{:S(2)}) copy-start(bf16[5,45,1440]{2,0,1:T(8,128)(2,1)} %copy-done.5) | copy-start | bytes 1944004
  235.4 1.2 copy-start
  383.3 2.0 copy-start.1
  385.8 25.0 %collective-permute-start.7 = (bf16[1,160,128]{2,1,0:T(8,128)(2,1)S(1)}, bf16[1,160,128]{2,1,0:T(8,128)(2,1)S(1)}, u32[]{:S(2)}, u32[]{:S(2)}) collective-permute-start(bf16[1,160,128]{2,1,0:T(8,128)(2,1)S(1)} %get-tuple-element.7), channel_id=1, source_target_pairs={{8,0},{16,8},{24,16},{32,24},{40,32},{48,40},{56,48},{64,56},{72,6... | collective-permute-start | bytes 122888 | tf_op jit(solution)/shard_map/ppermute | solution.py:21
  386.2 24.6 %collective-permute-start.8 = (bf16[1,160,128]{2,1,0:T(8,128)(2,1)S(1)}, bf16[1,160,128]{2,1,0:T(8,128)(2,1)S(1)}, u32[]{:S(2)}, u32[]{:S(2)}) collective-permute-start(bf16[1,160,128]{2,1,0:T(8,128)(2,1)S(1)} %get-tuple-element.8), channel_id=1, source_target_pairs={{0,8},{8,16},{16,24},{24,32},{32,40},{40,48},{48,56},{56,64},{64,7... | collective-permute-start | bytes 122888 | tf_op jit(solution)/shard_map/ppermute | solution.py:19
  388.9 22.0 %copy-start.4 = (f32[45,32,128]{2,1,0:T(8,128)S(1)}, f32[45,32,128]{2,1,0:T(8,128)}, u32[]{:S(2)}) copy-start(f32[45,32,128]{2,1,0:T(8,128)} %get-tuple-element.16) | copy-start | bytes 2211844
  391.2 9.8 %collective-permute-start.9 = (bf16[45,160,1]{1,0,2:T(8,128)(2,1)S(1)}, bf16[45,160,1]{1,0,2:T(8,128)(2,1)S(1)}, u32[]{:S(2)}, u32[]{:S(2)}) collective-permute-start(bf16[45,160,1]{1,0,2:T(8,128)(2,1)S(1)} %copy.63), channel_id=1, source_target_pairs={{1,0},{2,1},{3,2},{4,3},{5,4},{6,5},{7,6},{9,8},{10,9},{11,10},{12... | collective-permute-start | bytes 43208 | tf_op jit(solution)/shard_map/ppermute | solution.py:21
  398.9 9.4 %collective-permute-start.10 = (bf16[45,160,1]{1,0,2:T(8,128)(2,1)S(1)}, bf16[45,160,1]{1,0,2:T(8,128)(2,1)}, u32[]{:S(2)}, u32[]{:S(2)}) collective-permute-start(bf16[45,160,1]{1,0,2:T(8,128)(2,1)S(1)} %copy.65), channel_id=1, source_target_pairs={{0,1},{1,2},{2,3},{3,4},{4,5},{5,6},{6,7},{8,9},{9,10},{10,11},{11... | collective-permute-start | bytes 43208 | tf_op jit(solution)/shard_map/ppermute | solution.py:19
Sparse Core Ops, SparseCore 0:
  66.6 135.8 reduce-scatter.2
  250.3 132.9 reduce-scatter.4
